TPU v7x, 32 devices: a whole 2x2x4 slice. The times are simulated.
32 devices in a mesh: groups: 2 (over x), dp: 4 (over y, core), region: 4 (over z).
Axes of the slice: x: 2, y: 2, z: 4, core: 2. Of those that a mesh axis runs over, the one named last changes fastest.
Arguments:
- features: bfloat16 [8, 16384, 256], P(('groups', 'dp'), 'region'), parts along dimension 0, may hold values from -6 to 6
- adjacency: bfloat16 [8, 384, 128, 128], P(('groups', 'dp'), 'region'), parts along dimension 0, may hold values from -0.3125 to 0.3125
- src_tiles: int32 [8, 384], P(('groups', 'dp'), 'region'), parts along dimension 0, may hold values from 0 to 39, as said below
- dst_tiles: int32 [8, 384], P(('groups', 'dp'), 'region'), parts along dimension 0, may hold values from 0 to 31
- counts: int32 [8, 4], P(('groups', 'dp'), 'region'), parts along dimension 0, may hold values from 1 to 96, as said below
- send_low: int32 [8, 16], P(('groups', 'dp'), 'region'), parts along dimension 0, may hold values from 0 to 31, as said below
- send_high: int32 [8, 16], P(('groups', 'dp'), 'region'), parts along dimension 0, may hold values from 0 to 31, as said below
- w_message: bfloat16 [256, 256], replicated, may hold values from -0.375 to 0.375
- w_update: bfloat16 [256, 256], replicated, may hold values from -0.375 to 0.375
- grad_out: bfloat16 [8, 16384, 256], P(('groups', 'dp'), 'region'), parts along dimension 0, may hold values from -6 to 6
Outputs:
- output: bfloat16 [8, 16384, 256], P(('groups', 'dp'), 'region'), parts along dimension 0
- grad_features: bfloat16 [8, 16384, 256], P(('groups', 'dp'), 'region'), parts along dimension 0
- grad_message: float32 [512, 256], P('groups'), parts along dimension 0
- grad_update: float32 [512, 256], P('groups'), parts along dimension 0
There are 2 independent parts, one for each index of `groups`. A program takes and returns all parts, laid end to end along the dimension named above; an argument that names none is the same for every part. Nothing has to cross between parts.
Inputs may be any that keep to these rules, and one draw needn't show every extreme that they name: `src_tiles`: index into a region's extended list of 40 tiles. `counts`: in each event one region has all 96 slots live. `send_low`: the 4 entries of one region are distinct. `send_high`: the 4 entries of one region are distinct.
All inputs are finite; a program needn't handle non-finite values.
Results may differ from a plain program's by a relative error of at most 0.007.
Values may be sent and summed in bfloat16 or wider, within the bound.
A program may use at most 128 MiB of HBM per device.

v0:
```python
import math
import jax
import jax.numpy as jnp
from jax import lax
from jax.sharding import PartitionSpec as P


def with_halo(cells, sides, width):
    for axis, dim in sides:
        count = lax.axis_size(axis)
        head = lax.slice_in_dim(cells, 0, width, axis=dim)
        tail = lax.slice_in_dim(cells, cells.shape[dim] - width, cells.shape[dim], axis=dim)
        cells = jnp.concatenate(
            [
                lax.ppermute(tail, axis, [(i, (i + 1) % count) for i in range(count)]),
                cells,
                lax.ppermute(head, axis, [((i + 1) % count, i) for i in range(count)]),
            ],
            axis=dim,
        )
    return cells


def body(
    features,
    adjacency,
    src_tiles,
    dst_tiles,
    counts,
    send_low,
    send_high,
    w_message,
    w_update,
    grad_out,
):
    tile = adjacency.shape[-1]
    slots = adjacency.shape[1]
    width = features.shape[-1]
    x_rows = features[0]
    ntile = x_rows.shape[0] // tile
    bound = send_low.shape[1]
    lows = send_low[0]
    highs = send_high[0]
    message = jnp.dot(x_rows, w_message, preferred_element_type=jnp.float32).astype(jnp.bfloat16)
    msg_tiles = message.reshape(ntile, tile, width)
    rims = jnp.concatenate([msg_tiles[lows], msg_tiles[highs]], axis=0)
    padded = with_halo(rims, (("region", 0),), bound)
    halo_tiles = jnp.concatenate([padded[:bound], padded[-bound:]], axis=0)
    extended = jnp.concatenate([msg_tiles, halo_tiles], axis=0)
    live = (jnp.arange(slots) < counts[0, 0]).astype(jnp.float32)
    src = src_tiles[0]
    dst = dst_tiles[0]
    adj = adjacency[0]
    gathered = extended[src]
    contrib = jnp.einsum("kij,kjd->kid", adj, gathered, preferred_element_type=jnp.float32)
    aggregate = (
        jnp.zeros((ntile, tile, width), jnp.float32).at[dst].add(contrib * live[:, None, None])
    )
    aggregate = aggregate.astype(jnp.bfloat16).reshape(-1, width)
    update = jnp.dot(aggregate, w_update, preferred_element_type=jnp.float32)
    sig = jax.nn.sigmoid(update)
    output = (x_rows.astype(jnp.float32) + update * sig).astype(jnp.bfloat16)
    g_rows = grad_out[0]
    grad_in = (g_rows.astype(jnp.float32) * sig * (1.0 + update * (1.0 - sig))).astype(jnp.bfloat16)
    part_update = lax.dot_general(
        aggregate, grad_in, (((0,), (0,)), ((), ())), preferred_element_type=jnp.float32
    )
    grad_agg = lax.dot_general(
        grad_in, w_update, (((1,), (1,)), ((), ())), preferred_element_type=jnp.float32
    )
    grad_agg = grad_agg.astype(jnp.bfloat16).reshape(ntile, tile, width)
    picked = grad_agg[dst]
    back = jnp.einsum("kij,kid->kjd", adj, picked, preferred_element_type=jnp.float32)
    grad_ext = (
        jnp.zeros((ntile + 2 * bound, tile, width), jnp.float32)
        .at[src]
        .add(back * live[:, None, None])
    )
    rims_back = grad_ext[ntile:]
    padded_back = with_halo(rims_back, (("region", 0),), bound)
    from_lower = padded_back[:bound]
    from_upper = padded_back[-bound:]
    grad_msg = grad_ext[:ntile]
    grad_msg = grad_msg.at[lows].add(from_lower)
    grad_msg = grad_msg.at[highs].add(from_upper)
    grad_msg = grad_msg.astype(jnp.bfloat16).reshape(-1, width)
    part_message = lax.dot_general(
        x_rows, grad_msg, (((0,), (0,)), ((), ())), preferred_element_type=jnp.float32
    )
    grad_features = (
        g_rows.astype(jnp.float32)
        + lax.dot_general(
            grad_msg, w_message, (((1,), (1,)), ((), ())), preferred_element_type=jnp.float32
        )
    ).astype(jnp.bfloat16)
    sum_message, sum_update = lax.psum((part_message, part_update), ("dp", "region"))
    scale = 1.0 / math.sqrt(lax.axis_size("dp") * lax.axis_size("region") * x_rows.shape[0])
    return (output[None], grad_features[None], sum_message * scale, sum_update * scale)


def solution(mesh):
    in_specs = (
        P(("groups", "dp"), "region", None),
        P(("groups", "dp"), "region", None, None),
        P(("groups", "dp"), "region"),
        P(("groups", "dp"), "region"),
        P(("groups", "dp"), "region"),
        P(("groups", "dp"), "region"),
        P(("groups", "dp"), "region"),
        P(),
        P(),
        P(("groups", "dp"), "region", None),
    )
    out_specs = (
        P(("groups", "dp"), "region", None),
        P(("groups", "dp"), "region", None),
        P("groups", None),
        P("groups", None),
    )
    return jax.shard_map(body, mesh=mesh, in_specs=in_specs, out_specs=out_specs, check_vma=False)
```

profile of v0, /device:TPU:1, one launch (start us, length us, event | category | flops | bytes accessed | tf_op | source)
XLA Modules:
  0.0 307.1 jit_solution(6473691448623572954)
XLA Ops:
  7.2 0.0 copy-start
  7.2 0.0 copy-start.11
  7.2 0.0 all-reduce.3.cloned.1.call-start
  7.3 0.8 fusion.14
  8.1 3.7 %convolution_convert_fusion.1 = bf16[4096,256]{1,0:T(8,128)(2,1)} fusion(bf16[256,256]{1,0:T(8,128)(2,1)} %param.17, bf16[1,4096,256]{2,1,0:T(8,128)(2,1)} %param.10), kind=kOutput, calls=%fused_computation.14 | convolution fusion | flops 537919488 | bytes 4325376 | tf_op jit(solution)/shard_map/dot_general | solution.py:44
  11.8 2.9 gather_fusion
  14.7 2.1 collective-permute-start
  16.8 2.9 gather_fusion.1
  19.7 2.0 collective-permute-start.1
  22.4 2.6 collective-permute-done
  25.1 6.4 %collective-permute-done.1 = bf16[4,128,256]{2,1,0:T(8,128)(2,1)S(1)} collective-permute-done((bf16[4,128,256]{2,1,0:T(8,128)(2,1)}, bf16[4,128,256]{2,1,0:T(8,128)(2,1)S(1)}, u32[]{:S(2)}, u32[]{:S(2)}) %collective-permute-start.1) | collective-permute-done | bytes 262176 | tf_op jit(solution)/shard_map/ppermute | solution.py:17
  31.4 3.5 %pad_maximum_fusion = bf16[40,128,256]{2,1,0:T(8,128)(2,1)} fusion(bf16[4,128,256]{2,1,0:T(8,128)(2,1)S(1)} %collective-permute-done.1, bf16[4,128,256]{2,1,0:T(8,128)(2,1)S(1)} %collective-permute-done, bf16[32,128,256]{2,1,0:T(8,128)(2,1)} %bitcast.66), kind=kLoop, calls=%fused_computation.22 | loop fusion | flops 2621440 | bytes 5242880 | tf_op jit(solution)/shard_map/concatenate | solution.py:49
  34.9 7.7 %gather_fusion.2 = bf16[96,128,256]{2,1,0:T(8,128)(2,1)} fusion(bf16[40,128,256]{2,1,0:T(8,128)(2,1)} %pad_maximum_fusion, s32[1024]{0:T(1024)S(1)} %pad_clamp_fusion.1), kind=kCustom, calls=%fused_computation.2 | custom fusion | bytes 12583296 | tf_op jit(solution)/shard_map/gather | solution.py:54
  42.6 9.8 %multiply_bitcast_fusion.1 = f32[96,128,256]{1,2,0:T(8,128)} fusion(f32[96]{0:T(128)S(1)} %compare_convert_fusion, bf16[96,128,256]{2,1,0:T(8,128)(2,1)} %gather_fusion.2, bf16[1,96,128,128]{3,2,1,0:T(8,128)(2,1)S(1)} %copy-done), kind=kOutput, calls=%fused_computation.9 | convolution fusion | flops 808452096 | bytes 22020480 | tf_op jit(solution)/shard_map/kij,kjd->kid/dot_general | solution.py:55
  52.5 12.6 %copy.20 = f32[96,128,256]{2,1,0:T(8,128)} copy(f32[96,128,256]{1,2,0:T(8,128)} %multiply_bitcast_fusion.1) | data formatting | bytes 25165824 | tf_op jit(solution)/shard_map/mul | solution.py:57
  65.1 2.4 broadcast_in_dim.8
  67.5 28.6 %scatter_fusion = f32[32,128,256]{2,1,0:T(8,128)} fusion(f32[32,128,256]{2,1,0:T(8,128)} %broadcast_in_dim.8, s32[96]{0:T(128)S(1)} %fusion.13, f32[96,128,256]{2,1,0:T(8,128)} %copy.20), kind=kCustom, calls=%fused_computation.4 | custom fusion | flops 3145728 | bytes 37749120 | tf_op jit(solution)/shard_map/scatter-add | solution.py:57
  96.1 2.6 convert_element_type.41
  98.7 0.2 copy-done.3
  98.9 0.6 copy-done.6
  99.6 3.6 %fusion.3 = (bf16[4096,256]{1,0:T(8,128)(2,1)S(1)}, bf16[1,4096,256]{2,1,0:T(8,128)(2,1)}) fusion(bf16[1,4096,256]{2,1,0:T(8,128)(2,1)S(1)} %copy-done.6, bf16[1,4096,256]{2,1,0:T(8,128)(2,1)S(1)} %copy-done.3, bf16[4096,256]{1,0:T(8,128)(2,1)S(1)} %bitcast.69, bf16[256,256]{1,0:T(8,128)(2,1)S(1)} %copy-done.10), kind=kOutput, calls=%fused_computation.17 | convolution fusion | flops 551550976 | bytes 10616832 | tf_op jit(solution)/shard_map/dot_general | solution.py:60
  103.2 1.3 copy-done.4
  104.5 2.1 convolution_convert_fusion
  106.6 7.6 %gather_fusion.3 = bf16[96,128,256]{2,1,0:T(8,128)(2,1)} fusion(bf16[32,128,256]{2,1,0:T(8,128)(2,1)} %bitcast.63, s32[1024]{0:T(1024)S(1)} %pad_clamp_fusion), kind=kCustom, calls=%fused_computation.3 | custom fusion | bytes 12583296 | tf_op jit(solution)/shard_map/gather | solution.py:72
  114.2 9.8 %multiply_bitcast_fusion = f32[96,128,256]{1,2,0:T(8,128)} fusion(f32[96]{0:T(128)S(1)} %compare_convert_fusion, bf16[96,128,256]{2,1,0:T(8,128)(2,1)} %gather_fusion.3, bf16[1,96,128,128]{3,2,1,0:T(8,128)(2,1)S(1)} %copy-done), kind=kOutput, calls=%fused_computation.8 | convolution fusion | flops 808452096 | bytes 22020480 | tf_op jit(solution)/shard_map/kij,kid->kjd/dot_general | solution.py:73
  124.0 12.6 %copy.22 = f32[96,128,256]{2,1,0:T(8,128)} copy(f32[96,128,256]{1,2,0:T(8,128)} %multiply_bitcast_fusion) | data formatting | bytes 25165824 | tf_op jit(solution)/shard_map/mul | solution.py:77
  136.6 2.9 broadcast_in_dim.10
  139.5 28.5 %scatter_fusion.1 = f32[40,128,256]{2,1,0:T(8,128)} fusion(f32[40,128,256]{2,1,0:T(8,128)} %broadcast_in_dim.10, s32[96]{0:T(128)S(1)} %fusion.16, f32[96,128,256]{2,1,0:T(8,128)} %copy.22), kind=kCustom, calls=%fused_computation.5 | custom fusion | flops 3145728 | bytes 37749120 | tf_op jit(solution)/shard_map/scatter-add | solution.py:77
  168.0 2.1 fusion.17
  170.1 0.4 collective-permute-start.2
  170.5 2.8 collective-permute-start.3
  173.4 4.6 %slice.23 = f32[32,128,256]{2,1,0:T(8,128)} slice(f32[40,128,256]{2,1,0:T(8,128)} %scatter_fusion.1), slice={[0:32], [0:128], [0:256]} | slice | bytes 8388608 | tf_op jit(solution)/shard_map/slice | solution.py:83
  178.0 1.6 fusion.18
  179.6 5.7 %collective-permute-done.2 = f32[4,128,256]{2,1,0:T(8,128)S(1)} collective-permute-done((f32[4,128,256]{2,1,0:T(8,128)S(1)}, f32[4,128,256]{2,1,0:T(8,128)S(1)}, u32[]{:S(2)}, u32[]{:S(2)}) %collective-permute-start.2) | collective-permute-done | bytes 524320 | tf_op jit(solution)/shard_map/ppermute | solution.py:15
  185.3 2.6 scatter_fusion.2
  188.0 6.7 %collective-permute-done.3 = f32[4,128,256]{2,1,0:T(8,128)S(1)} collective-permute-done((f32[4,128,256]{2,1,0:T(8,128)}, f32[4,128,256]{2,1,0:T(8,128)S(1)}, u32[]{:S(2)}, u32[]{:S(2)}) %collective-permute-start.3) | collective-permute-done | bytes 524320 | tf_op jit(solution)/shard_map/ppermute | solution.py:17
  194.7 2.6 scatter_fusion.3
  197.3 2.5 convert_element_type.47
  199.8 0.0 copy-start.9
  199.8 1.3 copy-done.2
  201.1 3.0 fusion.10
  204.1 0.0 all-reduce.3.cloned.1.call-update
  204.2 0.0 copy-start.1
  204.2 4.4 %fusion.1 = bf16[1,4096,256]{2,1,0:T(8,128)(2,1)} fusion(bf16[4096,256]{1,0:T(8,128)(2,1)} %bitcast.68, bf16[256,256]{1,0:T(8,128)(2,1)S(1)} %copy-done.9, bf16[1,4096,256]{2,1,0:T(8,128)(2,1)} %param.19), kind=kOutput, calls=%fused_computation.15 | convolution fusion | flops 540016640 | bytes 6422528 | tf_op jit(solution)/shard_map/dot_general | solution.py:92
  208.6 87.2 %all-reduce.3.cloned.1.call-done = (f32[256,256]{0,1:T(8,128)}, f32[256,256]{0,1:T(8,128)}) async-done(((f32[256,256]{0,1:T(8,128)}, f32[256,256]{0,1:T(8,128)}), (f32[256,256]{0,1:T(8,128)}, f32[256,256]{0,1:T(8,128)})) %all-reduce.3.cloned.1.call-update) | async-done | bytes 524304 | tf_op jit(solution)/shard_map/psum | solution.py:96
  295.9 1.8 broadcast_multiply_fusion
  297.6 1.8 copy.24
  299.4 0.8 copy.25
  (28 shorter events, 0.1 us)
Async XLA Ops:
  7.2 35.5 %copy-start = (bf16[1,96,128,128]{3,2,1,0:T(8,128)(2,1)S(1)}, bf16[1,96,128,128]{3,2,1,0:T(8,128)(2,1)}, u32[]{:S(2)}) copy-start(bf16[1,96,128,128]{3,2,1,0:T(8,128)(2,1)} %param.11) | copy-start | bytes 9437188
  7.2 9.6 %copy-start.11 = (s32[1,4]{1,0:T(1,128)S(1)}, s32[1,4]{1,0:T(1,128)}, u32[]{:S(2)}) copy-start(s32[1,4]{1,0:T(1,128)} %param.15) | copy-start | bytes 52
  7.2 14.5 %copy-start.12 = (s32[1,96]{1,0:T(1,128)S(1)}, s32[1,96]{1,0:T(1,128)}, u32[]{:S(2)}) copy-start(s32[1,96]{1,0:T(1,128)} %param.12) | copy-start | bytes 1156
  7.2 15.2 %copy-start.13 = (s32[1,96]{1,0:T(1,128)S(1)}, s32[1,96]{1,0:T(1,128)}, u32[]{:S(2)}) copy-start(s32[1,96]{1,0:T(1,128)} %param.13) | copy-start | bytes 1156
  7.2 288.6 %all-reduce.3.cloned.1.call-start = ((), (), s32[]{:S(2)}) async-start(), calls=%async_computation | async-start | bytes 1048576 | tf_op jit(solution)/shard_map/psum | solution.py:96
  14.7 10.4 %collective-permute-start = (bf16[4,128,256]{2,1,0:T(8,128)(2,1)}, bf16[4,128,256]{2,1,0:T(8,128)(2,1)S(1)}, u32[]{:S(2)}, u32[]{:S(2)}) collective-permute-start(bf16[4,128,256]{2,1,0:T(8,128)(2,1)} %gather_fusion), channel_id=1, source_target_pairs={{0,1},{1,2},{2,3},{3,0},{4,5},{5,6},{6,7},{7,4},{8,9},{9,10},{10,1... | collective-permute-start | bytes 786440 | tf_op jit(solution)/shard_map/ppermute | solution.py:15
  19.7 11.7 %collective-permute-start.1 = (bf16[4,128,256]{2,1,0:T(8,128)(2,1)}, bf16[4,128,256]{2,1,0:T(8,128)(2,1)S(1)}, u32[]{:S(2)}, u32[]{:S(2)}) collective-permute-start(bf16[4,128,256]{2,1,0:T(8,128)(2,1)} %gather_fusion.1), channel_id=1, source_target_pairs={{1,0},{2,1},{3,2},{0,3},{5,4},{6,5},{7,6},{4,7},{9,8},{10,9},{11,1... | collective-permute-start | bytes 786440 | tf_op jit(solution)/shard_map/ppermute | solution.py:17
  96.1 2.9 copy-start.3
  96.1 3.5 %copy-start.6 = (bf16[1,4096,256]{2,1,0:T(8,128)(2,1)S(1)}, bf16[1,4096,256]{2,1,0:T(8,128)(2,1)}, u32[]{:S(2)}) copy-start(bf16[1,4096,256]{2,1,0:T(8,128)(2,1)} %param.19) | copy-start | bytes 6291460
  96.1 3.5 %copy-start.10 = (bf16[256,256]{1,0:T(8,128)(2,1)S(1)}, bf16[256,256]{1,0:T(8,128)(2,1)}, u32[]{:S(2)}) copy-start(bf16[256,256]{1,0:T(8,128)(2,1)} %param.18) | copy-start | bytes 393220
  98.7 4.5 %copy-start.7 = (bf16[32,128,256]{2,1,0:T(8,128)(2,1)}, bf16[32,128,256]{2,1,0:T(8,128)(2,1)S(1)}, u32[]{:S(2)}) copy-start(bf16[32,128,256]{2,1,0:T(8,128)(2,1)S(1)} %convert_element_type.41) | copy-start | bytes 6291460
  103.2 1.3 copy-start.4
  170.1 15.2 %collective-permute-start.2 = (f32[4,128,256]{2,1,0:T(8,128)S(1)}, f32[4,128,256]{2,1,0:T(8,128)S(1)}, u32[]{:S(2)}, u32[]{:S(2)}) collective-permute-start(f32[4,128,256]{2,1,0:T(8,128)S(1)} %get-tuple-element.15), channel_id=1, source_target_pairs={{0,1},{1,2},{2,3},{3,0},{4,5},{5,6},{6,7},{7,4},{8,9},{9,10},{10,1... | collective-permute-start | bytes 1572872 | tf_op jit(solution)/shard_map/ppermute | solution.py:15
  170.5 7.4 %copy-start.5 = (bf16[4096,256]{1,0:T(8,128)(2,1)S(1)}, bf16[4096,256]{1,0:T(8,128)(2,1)}, u32[]{:S(2)}) copy-start(bf16[4096,256]{1,0:T(8,128)(2,1)} %copy-done.4) | copy-start | bytes 6291460
  170.5 7.4 %copy-start.8 = (bf16[32,128,256]{2,1,0:T(8,128)(2,1)S(1)}, bf16[32,128,256]{2,1,0:T(8,128)(2,1)}, u32[]{:S(2)}) copy-start(bf16[32,128,256]{2,1,0:T(8,128)(2,1)} %copy-done.7) | copy-start | bytes 6291460
  170.5 24.1 %collective-permute-start.3 = (f32[4,128,256]{2,1,0:T(8,128)}, f32[4,128,256]{2,1,0:T(8,128)S(1)}, u32[]{:S(2)}, u32[]{:S(2)}) collective-permute-start(f32[4,128,256]{2,1,0:T(8,128)} %get-tuple-element.14), channel_id=1, source_target_pairs={{1,0},{2,1},{3,2},{0,3},{5,4},{6,5},{7,6},{4,7},{9,8},{10,9},{11,1... | collective-permute-start | bytes 1572872 | tf_op jit(solution)/shard_map/ppermute | solution.py:17
  199.8 1.3 copy-start.2
  199.8 4.4 %copy-start.9 = (bf16[256,256]{1,0:T(8,128)(2,1)S(1)}, bf16[256,256]{1,0:T(8,128)(2,1)}, u32[]{:S(2)}) copy-start(bf16[256,256]{1,0:T(8,128)(2,1)} %param.17) | copy-start | bytes 393220
  204.2 96.1 %copy-start.1 = (bf16[1,96,128,128]{3,2,1,0:T(8,128)(2,1)S(1)}, bf16[1,96,128,128]{3,2,1,0:T(8,128)(2,1)}, u32[]{:S(2)}) copy-start(bf16[1,96,128,128]{3,2,1,0:T(8,128)(2,1)} %param.11) | copy-start | bytes 9437188
Sparse Core Ops, SparseCore 0:
  204.3 91.5 all-reduce.2
where the time goes:
time: 308 us; the launch traced here: 307 us
  waiting for transfers between devices  109 us (35%)
  other arithmetic  73.6 us (24%)
  local copies, waits for them, and re-layouts  64.3 us (21%)
  matrix products  38.2 us (12%)
  between operations  14.8 us (5%)
  starting transfers between devices  7.47 us (2%)
    psum x1, waiting for transfers between devices, body(): lax.psum((part_message, part_update), ('dp', 'region'))  87.2 us
    scatter-add x1, other arithmetic, body(): jnp.zeros((ntile, tile, width), jnp.float32).at[dst]  28.6 us
    scatter-add x1, other arithmetic, body(): grad_ext = jnp.zeros((ntile + 2 * bound, tile, width), jnp.float32).at[sr...  28.5 us
    ppermute x2, waiting for transfers between devices, with_halo(): lax.ppermute(head, axis, [((i + 1) % count, i) for i in range(count)])  13 us
    mul x1, local copies, waits for them, and re-layouts, body(): contrib * live[:, None, None]  12.6 us
    mul x1, local copies, waits for them, and re-layouts, body(): back * live[:, None, None]  12.6 us
    dot_general x1, matrix products, body(): jnp.einsum('kij,kjd->kid', adj, gathered, preferred_element_type=jnp.floa...  9.84 us
    dot_general x1, matrix products, body(): jnp.einsum('kij,kid->kjd', adj, picked, preferred_element_type=jnp.float32)  9.84 us
  transfers between devices with their start and end apart: 5, of which 5 were waited for; matrix products, arithmetic and copies ran while one was open for 5% of the time, Pallas kernels for 0%

commit v1 on v0

--- a/solution.py
+++ b/solution.py
@@ -33,6 +33,12 @@
     w_update,
     grad_out,
 ):
+
+    def move_weights_for(inp, bus_axis, axis_name):
+        for s in (bus_axis, axis_name):
+            inp = lax.psum(inp, s)
+        return inp
+
     tile = adjacency.shape[-1]
     slots = adjacency.shape[1]
     width = features.shape[-1]
@@ -93,7 +99,7 @@
             grad_msg, w_message, (((1,), (1,)), ((), ())), preferred_element_type=jnp.float32
         )
     ).astype(jnp.bfloat16)
-    sum_message, sum_update = lax.psum((part_message, part_update), ("dp", "region"))
+    sum_message, sum_update = move_weights_for((part_message, part_update), "region", "dp")
     scale = 1.0 / math.sqrt(lax.axis_size("dp") * lax.axis_size("region") * x_rows.shape[0])
     return (output[None], grad_features[None], sum_message * scale, sum_update * scale)
 

time: 308 us -> 292 us (0.948)
  waiting for transfers between devices: 109 us -> 90.5 us
    psum x1 -> x2, waiting for transfers between devices: 87.2 us -> 69.3 us  [move_weights_for(): inp = lax.psum(inp, s)]
  transfers between devices with their start and end apart: 5 -> 6, of which waited for: 5 -> 6; matrix products, arithmetic and copies ran while one was open for 5% -> 6% of each run, Pallas kernels for 0% -> 0%
where the time goes in v1:
time: 292 us; the launch traced here: 289 us
  waiting for transfers between devices  90.5 us (31%)
  other arithmetic  73.8 us (25%)
  local copies, waits for them, and re-layouts  64.4 us (22%)
  matrix products  38.2 us (13%)
  between operations  14.8 us (5%)
  starting transfers between devices  7.51 us (3%)
    psum x2, waiting for transfers between devices, move_weights_for(): inp = lax.psum(inp, s)  69.3 us
    scatter-add x1, other arithmetic, body(): grad_ext = jnp.zeros((ntile + 2 * bound, tile, width), jnp.float32).at[sr...  28.7 us
    scatter-add x1, other arithmetic, body(): jnp.zeros((ntile, tile, width), jnp.float32).at[dst]  28.6 us
    ppermute x2, waiting for transfers between devices, with_halo(): lax.ppermute(head, axis, [((i + 1) % count, i) for i in range(count)])  12.6 us
    mul x1, local copies, waits for them, and re-layouts, body(): contrib * live[:, None, None]  12.6 us
    mul x1, local copies, waits for them, and re-layouts, body(): back * live[:, None, None]  12.6 us
    dot_general x1, matrix products, body(): jnp.einsum('kij,kjd->kid', adj, gathered, preferred_element_type=jnp.floa...  9.85 us
    dot_general x1, matrix products, body(): jnp.einsum('kij,kid->kjd', adj, picked, preferred_element_type=jnp.float32)  9.85 us
  transfers between devices with their start and end apart: 6, of which 6 were waited for; matrix products, arithmetic and copies ran while one was open for 6% of the time, Pallas kernels for 0%

profile of v1, /device:TPU:1, one launch (start us, length us, event | category | flops | bytes accessed | tf_op | source)
XLA Modules:
  0.0 289.2 jit_solution(12038763260572393632)
XLA Ops:
  7.2 0.0 copy-start
  7.2 0.0 all-reduce.5.cloned.1.call-start
  7.3 0.8 fusion.14
  8.1 3.7 %convolution_convert_fusion.1 = bf16[4096,256]{1,0:T(8,128)(2,1)} fusion(bf16[256,256]{1,0:T(8,128)(2,1)} %param.17, bf16[1,4096,256]{2,1,0:T(8,128)(2,1)} %param.10), kind=kOutput, calls=%fused_computation.14 | convolution fusion | flops 537919488 | bytes 4325376 | tf_op jit(solution)/shard_map/dot_general | solution.py:50
  11.8 2.9 gather_fusion
  14.7 2.1 collective-permute-start
  16.8 2.9 gather_fusion.1
  19.7 2.0 collective-permute-start.1
  22.4 2.6 collective-permute-done
  25.1 6.4 %collective-permute-done.1 = bf16[4,128,256]{2,1,0:T(8,128)(2,1)S(1)} collective-permute-done((bf16[4,128,256]{2,1,0:T(8,128)(2,1)}, bf16[4,128,256]{2,1,0:T(8,128)(2,1)S(1)}, u32[]{:S(2)}, u32[]{:S(2)}) %collective-permute-start.1) | collective-permute-done | bytes 262176 | tf_op jit(solution)/shard_map/ppermute | solution.py:17
  31.4 3.5 %pad_maximum_fusion = bf16[40,128,256]{2,1,0:T(8,128)(2,1)} fusion(bf16[4,128,256]{2,1,0:T(8,128)(2,1)S(1)} %collective-permute-done.1, bf16[4,128,256]{2,1,0:T(8,128)(2,1)S(1)} %collective-permute-done, bf16[32,128,256]{2,1,0:T(8,128)(2,1)} %bitcast.66), kind=kLoop, calls=%fused_computation.22 | loop fusion | flops 2621440 | bytes 5242880 | tf_op jit(solution)/shard_map/concatenate | solution.py:55
  34.9 7.7 %gather_fusion.2 = bf16[96,128,256]{2,1,0:T(8,128)(2,1)} fusion(bf16[40,128,256]{2,1,0:T(8,128)(2,1)} %pad_maximum_fusion, s32[1024]{0:T(1024)S(1)} %pad_clamp_fusion.1), kind=kCustom, calls=%fused_computation.2 | custom fusion | bytes 12583296 | tf_op jit(solution)/shard_map/gather | solution.py:60
  42.6 9.9 %multiply_bitcast_fusion.1 = f32[96,128,256]{1,2,0:T(8,128)} fusion(f32[96]{0:T(128)S(1)} %compare_convert_fusion, bf16[96,128,256]{2,1,0:T(8,128)(2,1)} %gather_fusion.2, bf16[1,96,128,128]{3,2,1,0:T(8,128)(2,1)S(1)} %copy-done), kind=kOutput, calls=%fused_computation.9 | convolution fusion | flops 808452096 | bytes 22020480 | tf_op jit(solution)/shard_map/kij,kjd->kid/dot_general | solution.py:61
  52.5 12.6 %copy.20 = f32[96,128,256]{2,1,0:T(8,128)} copy(f32[96,128,256]{1,2,0:T(8,128)} %multiply_bitcast_fusion.1) | data formatting | bytes 25165824 | tf_op jit(solution)/shard_map/mul | solution.py:63
  65.0 2.4 broadcast_in_dim.8
  67.5 28.6 %scatter_fusion = f32[32,128,256]{2,1,0:T(8,128)} fusion(f32[32,128,256]{2,1,0:T(8,128)} %broadcast_in_dim.8, s32[96]{0:T(128)S(1)} %fusion.13, f32[96,128,256]{2,1,0:T(8,128)} %copy.20), kind=kCustom, calls=%fused_computation.4 | custom fusion | flops 3145728 | bytes 37749120 | tf_op jit(solution)/shard_map/scatter-add | solution.py:63
  96.1 2.6 convert_element_type.41
  98.7 0.2 copy-done.3
  99.0 0.6 copy-done.6
  99.6 3.6 %fusion.3 = (bf16[4096,256]{1,0:T(8,128)(2,1)S(1)}, bf16[1,4096,256]{2,1,0:T(8,128)(2,1)}) fusion(bf16[1,4096,256]{2,1,0:T(8,128)(2,1)S(1)} %copy-done.6, bf16[1,4096,256]{2,1,0:T(8,128)(2,1)S(1)} %copy-done.3, bf16[4096,256]{1,0:T(8,128)(2,1)S(1)} %bitcast.69, bf16[256,256]{1,0:T(8,128)(2,1)S(1)} %copy-done.10), kind=kOutput, calls=%fused_computation.17 | convolution fusion | flops 551550976 | bytes 10616832 | tf_op jit(solution)/shard_map/dot_general | solution.py:66
  103.2 1.3 copy-done.4
  104.5 2.1 convolution_convert_fusion
  106.6 7.6 %gather_fusion.3 = bf16[96,128,256]{2,1,0:T(8,128)(2,1)} fusion(bf16[32,128,256]{2,1,0:T(8,128)(2,1)} %bitcast.63, s32[1024]{0:T(1024)S(1)} %pad_clamp_fusion), kind=kCustom, calls=%fused_computation.3 | custom fusion | bytes 12583296 | tf_op jit(solution)/shard_map/gather | solution.py:78
  114.2 9.9 %multiply_bitcast_fusion = f32[96,128,256]{1,2,0:T(8,128)} fusion(f32[96]{0:T(128)S(1)} %compare_convert_fusion, bf16[96,128,256]{2,1,0:T(8,128)(2,1)} %gather_fusion.3, bf16[1,96,128,128]{3,2,1,0:T(8,128)(2,1)S(1)} %copy-done), kind=kOutput, calls=%fused_computation.8 | convolution fusion | flops 808452096 | bytes 22020480 | tf_op jit(solution)/shard_map/kij,kid->kjd/dot_general | solution.py:79
  124.1 12.6 %copy.22 = f32[96,128,256]{2,1,0:T(8,128)} copy(f32[96,128,256]{1,2,0:T(8,128)} %multiply_bitcast_fusion) | data formatting | bytes 25165824 | tf_op jit(solution)/shard_map/mul | solution.py:83
  136.6 2.9 broadcast_in_dim.10
  139.5 28.7 %scatter_fusion.1 = f32[40,128,256]{2,1,0:T(8,128)} fusion(f32[40,128,256]{2,1,0:T(8,128)} %broadcast_in_dim.10, s32[96]{0:T(128)S(1)} %fusion.16, f32[96,128,256]{2,1,0:T(8,128)} %copy.22), kind=kCustom, calls=%fused_computation.5 | custom fusion | flops 3145728 | bytes 37749120 | tf_op jit(solution)/shard_map/scatter-add | solution.py:83
  168.2 2.1 fusion.17
  170.3 0.3 collective-permute-start.2
  170.6 3.0 %collective-permute-start.3 = (f32[4,128,256]{2,1,0:T(8,128)}, f32[4,128,256]{2,1,0:T(8,128)S(1)}, u32[]{:S(2)}, u32[]{:S(2)}) collective-permute-start(f32[4,128,256]{2,1,0:T(8,128)} %get-tuple-element.16), channel_id=1, source_target_pairs={{1,0},{2,1},{3,2},{0,3},{5,4},{6,5},{7,6},{4,7},{9,8},{10,9},{11,1... | collective-permute-start | bytes 1572872 | tf_op jit(solution)/shard_map/ppermute | solution.py:17
  173.6 4.6 %slice.23 = f32[32,128,256]{2,1,0:T(8,128)} slice(f32[40,128,256]{2,1,0:T(8,128)} %scatter_fusion.1), slice={[0:32], [0:128], [0:256]} | slice | bytes 8388608 | tf_op jit(solution)/shard_map/slice | solution.py:89
  178.1 1.6 fusion.18
  179.8 5.9 %collective-permute-done.2 = f32[4,128,256]{2,1,0:T(8,128)S(1)} collective-permute-done((f32[4,128,256]{2,1,0:T(8,128)S(1)}, f32[4,128,256]{2,1,0:T(8,128)S(1)}, u32[]{:S(2)}, u32[]{:S(2)}) %collective-permute-start.2) | collective-permute-done | bytes 524320 | tf_op jit(solution)/shard_map/ppermute | solution.py:15
  185.7 2.7 scatter_fusion.2
  188.4 6.3 %collective-permute-done.3 = f32[4,128,256]{2,1,0:T(8,128)S(1)} collective-permute-done((f32[4,128,256]{2,1,0:T(8,128)}, f32[4,128,256]{2,1,0:T(8,128)S(1)}, u32[]{:S(2)}, u32[]{:S(2)}) %collective-permute-start.3) | collective-permute-done | bytes 524320 | tf_op jit(solution)/shard_map/ppermute | solution.py:17
  194.6 2.7 scatter_fusion.3
  197.3 2.5 convert_element_type.47
  199.8 1.3 copy-done.2
  201.1 3.0 %fusion.10 = f32[256,256]{0,1:T(8,128)} fusion(bf16[4096,256]{1,0:T(8,128)(2,1)S(1)} %bitcast.67, bf16[1,4096,256]{2,1,0:T(8,128)(2,1)} %param.10), kind=kOutput, calls=%fused_computation.27 | convolution fusion | flops 536870912 | bytes 4456448 | tf_op jit(solution)/shard_map/dot_general | solution.py:93
  204.1 0.0 all-reduce.5.cloned.1.call-update
  204.1 0.0 all-reduce.7.cloned.1.call-start
  204.2 38.5 %all-reduce.5.cloned.1.call-done = (f32[256,256]{0,1:T(8,128)}, f32[256,256]{0,1:T(8,128)}) async-done(((f32[256,256]{0,1:T(8,128)}, f32[256,256]{0,1:T(8,128)}), (f32[256,256]{0,1:T(8,128)}, f32[256,256]{0,1:T(8,128)})) %all-reduce.5.cloned.1.call-update) | async-done | bytes 524304 | tf_op jit(solution)/shard_map/psum | solution.py:39
  242.7 0.0 all-reduce.7.cloned.1.call-update
  242.7 4.4 %fusion.1 = bf16[1,4096,256]{2,1,0:T(8,128)(2,1)} fusion(bf16[4096,256]{1,0:T(8,128)(2,1)} %bitcast.68, bf16[256,256]{1,0:T(8,128)(2,1)S(1)} %copy-done.9, bf16[1,4096,256]{2,1,0:T(8,128)(2,1)} %param.19), kind=kOutput, calls=%fused_computation.15 | convolution fusion | flops 540016640 | bytes 6422528 | tf_op jit(solution)/shard_map/dot_general | solution.py:98
  247.2 30.8 %all-reduce.7.cloned.1.call-done = (f32[256,256]{0,1:T(8,128)}, f32[256,256]{0,1:T(8,128)}) async-done(((f32[256,256]{0,1:T(8,128)}, f32[256,256]{0,1:T(8,128)}), (f32[256,256]{0,1:T(8,128)}, f32[256,256]{0,1:T(8,128)})) %all-reduce.7.cloned.1.call-update) | async-done | bytes 524304 | tf_op jit(solution)/shard_map/psum | solution.py:39
  278.0 1.8 broadcast_multiply_fusion
  279.7 1.8 copy.24
  281.5 0.8 copy.25
  (31 shorter events, 0.1 us)
Async XLA Ops:
  7.2 35.4 %copy-start = (bf16[1,96,128,128]{3,2,1,0:T(8,128)(2,1)S(1)}, bf16[1,96,128,128]{3,2,1,0:T(8,128)(2,1)}, u32[]{:S(2)}) copy-start(bf16[1,96,128,128]{3,2,1,0:T(8,128)(2,1)} %param.11) | copy-start | bytes 9437188
  7.2 9.6 %copy-start.11 = (s32[1,4]{1,0:T(1,128)S(1)}, s32[1,4]{1,0:T(1,128)}, u32[]{:S(2)}) copy-start(s32[1,4]{1,0:T(1,128)} %param.15) | copy-start | bytes 52
  7.2 14.5 %copy-start.12 = (s32[1,96]{1,0:T(1,128)S(1)}, s32[1,96]{1,0:T(1,128)}, u32[]{:S(2)}) copy-start(s32[1,96]{1,0:T(1,128)} %param.12) | copy-start | bytes 1156
  7.2 15.2 %copy-start.13 = (s32[1,96]{1,0:T(1,128)S(1)}, s32[1,96]{1,0:T(1,128)}, u32[]{:S(2)}) copy-start(s32[1,96]{1,0:T(1,128)} %param.13) | copy-start | bytes 1156
  7.2 235.5 %all-reduce.5.cloned.1.call-start = ((), (), s32[]{:S(2)}) async-start(), calls=%async_computation | async-start | bytes 1048576 | tf_op jit(solution)/shard_map/psum | solution.py:39
  14.7 10.4 %collective-permute-start = (bf16[4,128,256]{2,1,0:T(8,128)(2,1)}, bf16[4,128,256]{2,1,0:T(8,128)(2,1)S(1)}, u32[]{:S(2)}, u32[]{:S(2)}) collective-permute-start(bf16[4,128,256]{2,1,0:T(8,128)(2,1)} %gather_fusion), channel_id=1, source_target_pairs={{0,1},{1,2},{2,3},{3,0},{4,5},{5,6},{6,7},{7,4},{8,9},{9,10},{10,1... | collective-permute-start | bytes 786440 | tf_op jit(solution)/shard_map/ppermute | solution.py:15
  19.7 11.7 %collective-permute-start.1 = (bf16[4,128,256]{2,1,0:T(8,128)(2,1)}, bf16[4,128,256]{2,1,0:T(8,128)(2,1)S(1)}, u32[]{:S(2)}, u32[]{:S(2)}) collective-permute-start(bf16[4,128,256]{2,1,0:T(8,128)(2,1)} %gather_fusion.1), channel_id=1, source_target_pairs={{1,0},{2,1},{3,2},{0,3},{5,4},{6,5},{7,6},{4,7},{9,8},{10,9},{11,1... | collective-permute-start | bytes 786440 | tf_op jit(solution)/shard_map/ppermute | solution.py:17
  96.1 2.9 copy-start.3
  96.1 3.5 %copy-start.6 = (bf16[1,4096,256]{2,1,0:T(8,128)(2,1)S(1)}, bf16[1,4096,256]{2,1,0:T(8,128)(2,1)}, u32[]{:S(2)}) copy-start(bf16[1,4096,256]{2,1,0:T(8,128)(2,1)} %param.19) | copy-start | bytes 6291460
  96.1 3.5 %copy-start.10 = (bf16[256,256]{1,0:T(8,128)(2,1)S(1)}, bf16[256,256]{1,0:T(8,128)(2,1)}, u32[]{:S(2)}) copy-start(bf16[256,256]{1,0:T(8,128)(2,1)} %param.18) | copy-start | bytes 393220
  98.7 4.5 %copy-start.7 = (bf16[32,128,256]{2,1,0:T(8,128)(2,1)}, bf16[32,128,256]{2,1,0:T(8,128)(2,1)S(1)}, u32[]{:S(2)}) copy-start(bf16[32,128,256]{2,1,0:T(8,128)(2,1)S(1)} %convert_element_type.41) | copy-start | bytes 6291460
  103.2 1.3 copy-start.4
  170.3 15.4 %collective-permute-start.2 = (f32[4,128,256]{2,1,0:T(8,128)S(1)}, f32[4,128,256]{2,1,0:T(8,128)S(1)}, u32[]{:S(2)}, u32[]{:S(2)}) collective-permute-start(f32[4,128,256]{2,1,0:T(8,128)S(1)} %get-tuple-element.17), channel_id=1, source_target_pairs={{0,1},{1,2},{2,3},{3,0},{4,5},{5,6},{6,7},{7,4},{8,9},{9,10},{10,1... | collective-permute-start | bytes 1572872 | tf_op jit(solution)/shard_map/ppermute | solution.py:15
  170.6 7.6 %copy-start.5 = (bf16[4096,256]{1,0:T(8,128)(2,1)S(1)}, bf16[4096,256]{1,0:T(8,128)(2,1)}, u32[]{:S(2)}) copy-start(bf16[4096,256]{1,0:T(8,128)(2,1)} %copy-done.4) | copy-start | bytes 6291460
  170.6 7.6 %copy-start.8 = (bf16[32,128,256]{2,1,0:T(8,128)(2,1)S(1)}, bf16[32,128,256]{2,1,0:T(8,128)(2,1)}, u32[]{:S(2)}) copy-start(bf16[32,128,256]{2,1,0:T(8,128)(2,1)} %copy-done.7) | copy-start | bytes 6291460
  170.6 24.1 %collective-permute-start.3 = (f32[4,128,256]{2,1,0:T(8,128)}, f32[4,128,256]{2,1,0:T(8,128)S(1)}, u32[]{:S(2)}, u32[]{:S(2)}) collective-permute-start(f32[4,128,256]{2,1,0:T(8,128)} %get-tuple-element.16), channel_id=1, source_target_pairs={{1,0},{2,1},{3,2},{0,3},{5,4},{6,5},{7,6},{4,7},{9,8},{10,9},{11,1... | collective-permute-start | bytes 1572872 | tf_op jit(solution)/shard_map/ppermute | solution.py:17
  199.7 1.3 copy-start.2
  199.8 42.9 %copy-start.9 = (bf16[256,256]{1,0:T(8,128)(2,1)S(1)}, bf16[256,256]{1,0:T(8,128)(2,1)}, u32[]{:S(2)}) copy-start(bf16[256,256]{1,0:T(8,128)(2,1)} %param.17) | copy-start | bytes 393220
  204.1 73.8 %all-reduce.7.cloned.1.call-start = ((), (), s32[]{:S(2)}) async-start(), calls=%async_computation.1 | async-start | bytes 1048576 | tf_op jit(solution)/shard_map/psum | solution.py:39
  242.7 39.7 %copy-start.1 = (bf16[1,96,128,128]{3,2,1,0:T(8,128)(2,1)S(1)}, bf16[1,96,128,128]{3,2,1,0:T(8,128)(2,1)}, u32[]{:S(2)}) copy-start(bf16[1,96,128,128]{3,2,1,0:T(8,128)(2,1)} %param.11) | copy-start | bytes 9437188
Sparse Core Ops, SparseCore 0:
  204.3 38.3 all-reduce.4
  245.1 32.8 all-reduce.6
